TPU v7x, 512 devices: a whole 4x8x8 slice. The times are simulated.
512 devices in a mesh: lon: 32 (over x, z_hi, core), lat: 16 (over y, z_lo).
Axes of the slice: x: 4, y: 8, z: 8 (z_hi: 4, z_lo: 2; z = z_hi * 2 + z_lo), core: 2. Of those that a mesh axis runs over, the one named last changes fastest.
Arguments:
- queries: bfloat16 [128, 512, 1536], P('lat', 'lon'), may hold values from -24 to 24
- keys: bfloat16 [128, 512, 1536], P('lat', 'lon'), may hold values from -24 to 24
- values: bfloat16 [128, 512, 1536], P('lat', 'lon'), may hold values from -6 to 6
- out_grad: bfloat16 [128, 512, 1536], P('lat', 'lon'), may hold values from -6 to 6
- neighbours: int32 [512, 5], replicated, may hold values from -1 to 511, as said below
- partner: int32 [2, 32], replicated, may hold values from 0 to 31, as said below
Outputs:
- attended: bfloat16 [128, 512, 1536], P('lat', 'lon')
- grad_queries: bfloat16 [128, 512, 1536], P('lat', 'lon')
- grad_keys: bfloat16 [128, 512, 1536], P('lat', 'lon')
- grad_values: bfloat16 [128, 512, 1536], P('lat', 'lon')
Inputs may be any that keep to these rules, and one draw needn't show every extreme that they name: `neighbours`: row t = b * 32 + s lists, in some order and padded with -1, distinct tiles: t itself always, and any of b * 32 + (s - 1) mod 32, b * 32 + (s + 1) mod 32, t - 32 where b > 0 and t + 32 where b < 15. Rows of the first and the last band list all of those that exist. Each row is a permutation of the strips, and partner[j, s] - s - 16 is -1, 0 or 1 modulo 32.
All inputs are finite; a program needn't handle non-finite values.
Results may differ from a plain program's by a relative error of at most 0.022.
Values may be sent and summed in bfloat16 or wider, within the bound.
A program may use at most 64 MiB of HBM per device.

v0:
```python
import jax
import jax.numpy as jnp
from jax import lax
from jax.sharding import PartitionSpec as P

DH = 128


def with_halo(cells, sides, width, closed):
    for axis, dim in sides:
        count = lax.axis_size(axis)
        ends = count if closed else count - 1
        head = lax.slice_in_dim(cells, 0, width, axis=dim)
        tail = lax.slice_in_dim(cells, cells.shape[dim] - width, cells.shape[dim], axis=dim)
        cells = jnp.concatenate(
            [
                lax.ppermute(tail, axis, [(i, (i + 1) % count) for i in range(ends)]),
                cells,
                lax.ppermute(head, axis, [((i + 1) % count, i) for i in range(ends)]),
            ],
            axis=dim,
        )
    return cells


def partner_2(x, axis, apart):
    return lax.ppermute(x, axis, [(i, i ^ 1 << apart) for i in range(lax.axis_size(axis))])


def body(queries, keys, values, out_grad, neighbours, partner):
    lat_count = lax.axis_size("lat")
    lon_count = lax.axis_size("lon")
    band_index = lax.axis_index("lat")
    strip_index = lax.axis_index("lon")
    tile_rows, tile_cols, feature_width = queries.shape
    tokens = tile_rows * tile_cols
    head_count = feature_width // DH
    scale = DH ** (-0.5)
    half_cycle = lon_count // 2
    top_bit = lon_count.bit_length() - 2
    query = queries.reshape(tokens, head_count, DH)
    cotan = out_grad.reshape(tokens, head_count, DH)
    polar_band = (band_index == 0) | (band_index == lat_count - 1)
    partner_row = jnp.where(band_index == 0, partner[0], partner[1])

    def tile_id(band_id, strip_id):
        return band_id * lon_count + strip_id

    west_strip = (strip_index - 1) % lon_count
    east_strip = (strip_index + 1) % lon_count
    opposite = (strip_index + half_cycle) % lon_count
    has_north = band_index > 0
    has_south = band_index < lat_count - 1
    my_id = tile_id(band_index, strip_index)
    west_id = tile_id(band_index, west_strip)
    east_id = tile_id(band_index, east_strip)
    north_id = jnp.where(has_north, my_id - lon_count, -7)
    south_id = jnp.where(has_south, my_id + lon_count, -7)
    candidates = jnp.stack([my_id, west_id, east_id, north_id, south_id])
    my_links = neighbours[my_id]
    present = jnp.any(candidates[:, None] == my_links[None, :], axis=1)
    present = jnp.concatenate([present, polar_band[None]])
    mask_bias = jnp.where(present, 0.0, -jnp.inf).astype(jnp.float32)
    pair_block = jnp.stack([keys, values]).reshape(1, 1, 2, tokens, feature_width)
    near = with_halo(pair_block, (("lon", 1), ("lat", 0)), 1, True)
    self_pair = near[1, 1]
    west_pair = near[1, 0]
    east_pair = near[1, 2]
    north_pair = near[0, 1]
    south_pair = near[2, 1]
    target = partner_row[opposite]
    differ = (target - opposite - half_cycle) % lon_count
    facing = jnp.where(differ == lon_count - 1, -1, differ)
    send_pair = jnp.where(facing == -1, west_pair, jnp.where(facing == 0, self_pair, east_pair))
    polar_pair = partner_2(send_pair, "lon", top_bit)
    stacked = jnp.stack([self_pair, west_pair, east_pair, north_pair, south_pair, polar_pair])
    near_keys = stacked[:, 0].reshape(6, tokens, head_count, DH)
    near_values = stacked[:, 1].reshape(6, tokens, head_count, DH)
    scores = (
        jnp.einsum("qhd,jkhd->hqjk", query, near_keys, preferred_element_type=jnp.float32) * scale
    )
    scores = scores + mask_bias[None, None, :, None]
    highest = jnp.max(scores, axis=(2, 3), keepdims=True)
    total = jnp.sum(jnp.exp(scores - highest), axis=(2, 3), keepdims=True)
    log_norm = highest + jnp.log(total)
    probability = jnp.exp(scores - log_norm)
    weights = probability.astype(jnp.bfloat16)
    attended = jnp.einsum(
        "hqjk,jkhd->qhd", weights, near_values, preferred_element_type=jnp.float32
    ).astype(jnp.bfloat16)
    delta = jnp.sum(cotan.astype(jnp.float32) * attended.astype(jnp.float32), axis=-1)
    dprob = jnp.einsum("qhd,jkhd->hqjk", cotan, near_values, preferred_element_type=jnp.float32)
    dscore = (probability * (dprob - delta.T[:, :, None, None])).astype(jnp.bfloat16)
    grad_query = (
        scale * jnp.einsum("hqjk,jkhd->qhd", dscore, near_keys, preferred_element_type=jnp.float32)
    ).astype(jnp.bfloat16)

    def tile_terms(first, count):
        score_part = lax.slice_in_dim(dscore, first, first + count, axis=2)
        weight_part = lax.slice_in_dim(weights, first, first + count, axis=2)
        key_part = jnp.einsum(
            "hqjk,qhd->jkhd", score_part, query, preferred_element_type=jnp.float32
        )
        value_part = jnp.einsum(
            "hqjk,qhd->jkhd", weight_part, cotan, preferred_element_type=jnp.float32
        )
        return jnp.stack([key_part, value_part], axis=1)

    polar_terms = tile_terms(5, 1)[0]
    returned = partner_2(polar_terms.astype(jnp.bfloat16), "lon", top_bit).astype(polar_terms.dtype)
    zeros_like = jnp.zeros_like(returned)
    self_term = tile_terms(0, 1)[0] + jnp.where(facing == 0, returned, zeros_like)
    cycle_terms = tile_terms(1, 2)
    west_term = cycle_terms[0] + jnp.where(facing == -1, returned, zeros_like)
    east_term = cycle_terms[1] + jnp.where(facing == 1, returned, zeros_like)
    cycle_block = jnp.stack([west_term, east_term])[None]
    cycle_back = with_halo(cycle_block.astype(jnp.bfloat16), (("lon", 1),), 1, True).astype(
        cycle_block.dtype
    )
    band_block = tile_terms(3, 2)[:, None]
    band_back = with_halo(band_block.astype(jnp.bfloat16), (("lat", 0),), 1, False).astype(
        band_block.dtype
    )
    summed = self_term + cycle_back[0, 0] + cycle_back[0, 3] + band_back[0, 0] + band_back[3, 0]
    key_sum = summed[0]
    value_sum = summed[1]
    grad_keys = (scale * key_sum).astype(jnp.bfloat16)
    grad_values = value_sum.astype(jnp.bfloat16)
    out_shape = (tile_rows, tile_cols, feature_width)
    return (
        attended.reshape(out_shape),
        grad_query.reshape(out_shape),
        grad_keys.reshape(out_shape),
        grad_values.reshape(out_shape),
    )


def solution(mesh):
    return jax.shard_map(
        body,
        mesh=mesh,
        in_specs=(
            P("lat", "lon", None),
            P("lat", "lon", None),
            P("lat", "lon", None),
            P("lat", "lon", None),
            P(),
            P(),
        ),
        out_specs=(
            P("lat", "lon", None),
            P("lat", "lon", None),
            P("lat", "lon", None),
            P("lat", "lon", None),
        ),
        check_vma=False,
    )
```

profile of v0, /device:TPU:24, one launch (start us, length us, event | category | flops | bytes accessed | tf_op | source)
XLA Modules:
  0.0 241.6 jit_solution(8895753844608702467)
XLA Ops:
  1.9 2.1 collective-permute-start
  3.9 12.6 %collective-permute-start.1 = (bf16[1,1,2,128,1536]{4,3,2,1,0:T(8,128)(2,1)S(1)}, bf16[1,1,2,128,1536]{4,3,2,1,0:T(8,128)(2,1)S(1)}, u32[]{:S(2)}, u32[]{:S(2)}) collective-permute-start(bf16[1,1,2,128,1536]{4,3,2,1,0:T(8,128)(2,1)S(1)} %pad_maximum_fusion.7), channel_id=1, source_target_pairs={{16,0},{32,16},{48,32},{64,48},{80,64},{96,80},{112,96},{128,112},... | collective-permute-start | bytes 2359304 | tf_op jit(solution)/shard_map/ppermute | solution.py:19
  16.5 7.9 %collective-permute-done = bf16[1,1,2,128,1536]{4,3,2,1,0:T(8,128)(2,1)S(1)} collective-permute-done((bf16[1,1,2,128,1536]{4,3,2,1,0:T(8,128)(2,1)S(1)}, bf16[1,1,2,128,1536]{4,3,2,1,0:T(8,128)(2,1)S(1)}, u32[]{:S(2)}, u32[]{:S(2)}) %collective-permute-start) | collective-permute-done | bytes 786464 | tf_op jit(solution)/shard_map/ppermute | solution.py:17
  24.4 10.1 %collective-permute-done.1 = bf16[1,1,2,128,1536]{4,3,2,1,0:T(8,128)(2,1)S(1)} collective-permute-done((bf16[1,1,2,128,1536]{4,3,2,1,0:T(8,128)(2,1)S(1)}, bf16[1,1,2,128,1536]{4,3,2,1,0:T(8,128)(2,1)S(1)}, u32[]{:S(2)}, u32[]{:S(2)}) %collective-permute-start.1) | collective-permute-done | bytes 786464 | tf_op jit(solution)/shard_map/ppermute | solution.py:19
  34.5 2.8 %pad_maximum_fusion = bf16[1,3,2,128,1536]{4,3,2,1,0:T(8,128)(2,1)} fusion(bf16[1,1,2,128,1536]{4,3,2,1,0:T(8,128)(2,1)S(1)} %collective-permute-done.1, bf16[1,1,1,128,1536]{4,3,2,1,0:T(8,128)(2,1)} %bitcast.195, bf16[1,1,1,128,1536]{4,3,2,1,0:T(8,128)(2,1)} %bitcast.199, bf16[1,1,2,128,1536]{4,3,2,1,0:T(8,128)(2,1)S(1)} %collective-permute-done), kind=kLoop, calls=%fused_computation.15 | loop fusion | flops 3538944 | bytes 4718592 | tf_op jit(solution)/shard_map/concatenate | solution.py:15
  37.3 2.0 collective-permute-start.2
  43.8 4.8 %collective-permute-start.3 = (bf16[1,3,2,128,1536]{4,3,2,1,0:T(8,128)(2,1)}, bf16[1,3,2,128,1536]{4,3,2,1,0:T(8,128)(2,1)S(1)}, u32[]{:S(2)}, u32[]{:S(2)}) collective-permute-start(bf16[1,3,2,128,1536]{4,3,2,1,0:T(8,128)(2,1)} %pad_maximum_fusion), channel_id=1, source_target_pairs={{1,0},{2,1},{3,2},{4,3},{5,4},{6,5},{7,6},{8,7},{9,8},{10,9},{11,1... | collective-permute-start | bytes 7077896 | tf_op jit(solution)/shard_map/ppermute | solution.py:19
  48.9 2.7 %collective-permute-start.4 = (bf16[2,128,1536]{2,1,0:T(8,128)(2,1)S(1)}, bf16[2,128,1536]{2,1,0:T(8,128)(2,1)S(1)}, u32[]{:S(2)}, u32[]{:S(2)}) collective-permute-start(bf16[2,128,1536]{2,1,0:T(8,128)(2,1)S(1)} %fusion.54), channel_id=1, source_target_pairs={{0,256},{16,272},{32,288},{48,304},{64,320},{80,336},{96,352},{112... | collective-permute-start | bytes 2359304 | tf_op jit(solution)/shard_map/ppermute | solution.py:27
  51.8 85.9 %collective-permute-done.2 = bf16[1,3,2,128,1536]{4,3,2,1,0:T(8,128)(2,1)} collective-permute-done((bf16[1,3,2,128,1536]{4,3,2,1,0:T(8,128)(2,1)}, bf16[1,3,2,128,1536]{4,3,2,1,0:T(8,128)(2,1)}, u32[]{:S(2)}, u32[]{:S(2)}) %collective-permute-start.2) | collective-permute-done | bytes 2359328 | tf_op jit(solution)/shard_map/ppermute | solution.py:17
  140.8 1.9 fusion.73
  142.7 2.4 %copy.97 = bf16[6,1,128,1536]{2,3,0,1:T(8,128)(2,1)} copy(bf16[6,1,128,1536]{3,2,1,0:T(8,128)(2,1)S(1)} %get-tuple-element.9) | data formatting | bytes 4718592 | tf_op jit(solution)/shard_map/slice | solution.py:78
  145.1 3.0 %copy.98 = bf16[6,1,128,1536]{2,3,0,1:T(8,128)(2,1)S(1)} copy(bf16[6,1,128,1536]{3,2,1,0:T(8,128)(2,1)} %get-tuple-element.8) | data formatting | bytes 4718592 | tf_op jit(solution)/shard_map/slice | solution.py:77
  154.2 1.9 fusion
  160.0 2.2 copy.102
  162.1 2.1 reshape.292
  165.5 5.1 %collective-permute-start.5 = (bf16[2,128,12,128]{3,1,2,0:T(8,128)(2,1)S(1)}, bf16[2,128,12,128]{3,1,2,0:T(8,128)(2,1)S(1)}, u32[]{:S(2)}, u32[]{:S(2)}) collective-permute-start(bf16[2,128,12,128]{3,1,2,0:T(8,128)(2,1)S(1)} %maximum_bitcast_fusion.3), channel_id=1, source_target_pairs={{0,256},{16,272},{32,288},{48,304},{64,320},{80,336},{96,352},{112... | collective-permute-start | bytes 2359304 | tf_op jit(solution)/shard_map/ppermute | solution.py:27
  173.7 2.5 %collective-permute-start.9 = (bf16[1,1,2,128,12,128]{5,3,4,2,1,0:T(8,128)(2,1)}, bf16[1,1,2,128,12,128]{5,3,4,2,1,0:T(8,128)(2,1)}, u32[]{:S(2)}, u32[]{:S(2)}) collective-permute-start(bf16[1,1,2,128,12,128]{5,3,4,2,1,0:T(8,128)(2,1)} %get-tuple-element.17), channel_id=1, source_target_pairs={{1,0},{2,1},{3,2},{4,3},{5,4},{6,5},{7,6},{8,7},{9,8},{10,9},{11,1... | collective-permute-start | bytes 2359304 | tf_op jit(solution)/shard_map/ppermute | solution.py:19
  176.2 3.4 %collective-permute-start.8 = (bf16[1,1,2,128,12,128]{5,3,4,2,1,0:T(8,128)(2,1)}, bf16[1,1,2,128,12,128]{5,3,4,2,1,0:T(8,128)(2,1)}, u32[]{:S(2)}, u32[]{:S(2)}) collective-permute-start(bf16[1,1,2,128,12,128]{5,3,4,2,1,0:T(8,128)(2,1)} %get-tuple-element.16), channel_id=1, source_target_pairs={{0,1},{1,2},{2,3},{3,4},{4,5},{5,6},{6,7},{7,8},{8,9},{9,10},{10,1... | collective-permute-start | bytes 2359304 | tf_op jit(solution)/shard_map/ppermute | solution.py:17
  180.3 8.0 %collective-permute-done.5 = bf16[2,128,12,128]{3,1,2,0:T(8,128)(2,1)S(1)} collective-permute-done((bf16[2,128,12,128]{3,1,2,0:T(8,128)(2,1)S(1)}, bf16[2,128,12,128]{3,1,2,0:T(8,128)(2,1)S(1)}, u32[]{:S(2)}, u32[]{:S(2)}) %collective-permute-start.5) | collective-permute-done | bytes 786464 | tf_op jit(solution)/shard_map/ppermute | solution.py:27
  190.0 8.5 %collective-permute-start.7 = (bf16[1,1,2,128,12,128]{5,3,4,2,1,0:T(8,128)(2,1)}, bf16[1,1,2,128,12,128]{5,3,4,2,1,0:T(8,128)(2,1)}, u32[]{:S(2)}, u32[]{:S(2)}) collective-permute-start(bf16[1,1,2,128,12,128]{5,3,4,2,1,0:T(8,128)(2,1)} %bitcast.65), channel_id=1, source_target_pairs={{16,0},{32,16},{48,32},{64,48},{80,64},{96,80},{112,96},{128,112},... | collective-permute-start | bytes 2359304 | tf_op jit(solution)/shard_map/ppermute | solution.py:19
  198.5 1.9 collective-permute-start.6
  208.7 11.7 %collective-permute-done.9 = bf16[1,1,2,128,12,128]{5,3,4,2,1,0:T(8,128)(2,1)} collective-permute-done((bf16[1,1,2,128,12,128]{5,3,4,2,1,0:T(8,128)(2,1)}, bf16[1,1,2,128,12,128]{5,3,4,2,1,0:T(8,128)(2,1)}, u32[]{:S(2)}, u32[]{:S(2)}) %collective-permute-start.9) | collective-permute-done | bytes 786464 | tf_op jit(solution)/shard_map/ppermute | solution.py:19
  221.7 14.9 %collective-permute-done.6 = bf16[1,1,2,128,12,128]{5,3,4,2,1,0:T(8,128)(2,1)} collective-permute-done((bf16[1,1,2,128,12,128]{5,3,4,2,1,0:T(8,128)(2,1)}, bf16[1,1,2,128,12,128]{5,3,4,2,1,0:T(8,128)(2,1)}, u32[]{:S(2)}, u32[]{:S(2)}) %collective-permute-start.6) | collective-permute-done | bytes 786464 | tf_op jit(solution)/shard_map/ppermute | solution.py:17
  236.6 2.2 fusion.19
  (87 shorter events, 37.3 us)
Async XLA Ops:
  0.6 42.7 %copy-start = (s32[512,5]{0,1:T(8,128)S(1)}, s32[512,5]{0,1:T(8,128)}, u32[]{:S(2)}) copy-start(s32[512,5]{0,1:T(8,128)} %param.10) | copy-start | bytes 30724
  1.8 37.5 %copy-start.18 = (s32[2,32]{1,0:T(2,128)S(1)}, s32[2,32]{1,0:T(2,128)}, u32[]{:S(2)}) copy-start(s32[2,32]{1,0:T(2,128)} %param.11) | copy-start | bytes 772
  1.9 38.8 %copy-start.16 = (bf16[8,16,1536]{2,1,0:T(8,128)(2,1)S(1)}, bf16[8,16,1536]{2,1,0:T(8,128)(2,1)}, u32[]{:S(2)}) copy-start(bf16[8,16,1536]{2,1,0:T(8,128)(2,1)} %param.9) | copy-start | bytes 1179652
  1.9 22.5 %collective-permute-start = (bf16[1,1,2,128,1536]{4,3,2,1,0:T(8,128)(2,1)S(1)}, bf16[1,1,2,128,1536]{4,3,2,1,0:T(8,128)(2,1)S(1)}, u32[]{:S(2)}, u32[]{:S(2)}) collective-permute-start(bf16[1,1,2,128,1536]{4,3,2,1,0:T(8,128)(2,1)S(1)} %pad_maximum_fusion.7), channel_id=1, source_target_pairs={{0,16},{16,32},{32,48},{48,64},{64,80},{80,96},{96,112},{112,128},... | collective-permute-start | bytes 2359304 | tf_op jit(solution)/shard_map/ppermute | solution.py:17
  3.9 30.5 %collective-permute-start.1 = (bf16[1,1,2,128,1536]{4,3,2,1,0:T(8,128)(2,1)S(1)}, bf16[1,1,2,128,1536]{4,3,2,1,0:T(8,128)(2,1)S(1)}, u32[]{:S(2)}, u32[]{:S(2)}) collective-permute-start(bf16[1,1,2,128,1536]{4,3,2,1,0:T(8,128)(2,1)S(1)} %pad_maximum_fusion.7), channel_id=1, source_target_pairs={{16,0},{32,16},{48,32},{64,48},{80,64},{96,80},{112,96},{128,112},... | collective-permute-start | bytes 2359304 | tf_op jit(solution)/shard_map/ppermute | solution.py:19
  37.3 11.5 %copy-start.6 = (bf16[8,16,1536]{2,1,0:T(8,128)(2,1)S(1)}, bf16[8,16,1536]{2,1,0:T(8,128)(2,1)}, u32[]{:S(2)}) copy-start(bf16[8,16,1536]{2,1,0:T(8,128)(2,1)} %param.8) | copy-start | bytes 1179652
  37.3 11.5 %copy-start.7 = (bf16[8,16,1536]{2,1,0:T(8,128)(2,1)S(1)}, bf16[8,16,1536]{2,1,0:T(8,128)(2,1)}, u32[]{:S(2)}) copy-start(bf16[8,16,1536]{2,1,0:T(8,128)(2,1)} %param.7) | copy-start | bytes 1179652
  37.3 100.4 %collective-permute-start.2 = (bf16[1,3,2,128,1536]{4,3,2,1,0:T(8,128)(2,1)}, bf16[1,3,2,128,1536]{4,3,2,1,0:T(8,128)(2,1)}, u32[]{:S(2)}, u32[]{:S(2)}) collective-permute-start(bf16[1,3,2,128,1536]{4,3,2,1,0:T(8,128)(2,1)} %pad_maximum_fusion), channel_id=1, source_target_pairs={{0,1},{1,2},{2,3},{3,4},{4,5},{5,6},{6,7},{7,8},{8,9},{9,10},{10,1... | collective-permute-start | bytes 7077896 | tf_op jit(solution)/shard_map/ppermute | solution.py:17
  43.8 96.9 %collective-permute-start.3 = (bf16[1,3,2,128,1536]{4,3,2,1,0:T(8,128)(2,1)}, bf16[1,3,2,128,1536]{4,3,2,1,0:T(8,128)(2,1)S(1)}, u32[]{:S(2)}, u32[]{:S(2)}) collective-permute-start(bf16[1,3,2,128,1536]{4,3,2,1,0:T(8,128)(2,1)} %pad_maximum_fusion), channel_id=1, source_target_pairs={{1,0},{2,1},{3,2},{4,3},{5,4},{6,5},{7,6},{8,7},{9,8},{10,9},{11,1... | collective-permute-start | bytes 7077896 | tf_op jit(solution)/shard_map/ppermute | solution.py:19
  48.9 91.8 %collective-permute-start.4 = (bf16[2,128,1536]{2,1,0:T(8,128)(2,1)S(1)}, bf16[2,128,1536]{2,1,0:T(8,128)(2,1)S(1)}, u32[]{:S(2)}, u32[]{:S(2)}) collective-permute-start(bf16[2,128,1536]{2,1,0:T(8,128)(2,1)S(1)} %fusion.54), channel_id=1, source_target_pairs={{0,256},{16,272},{32,288},{48,304},{64,320},{80,336},{96,352},{112... | collective-permute-start | bytes 2359304 | tf_op jit(solution)/shard_map/ppermute | solution.py:27
  151.4 7.3 %copy-start.1 = (bf16[12,128,6,128]{1,3,2,0:T(8,128)(2,1)}, bf16[12,128,6,128]{1,3,2,0:T(8,128)(2,1)S(1)}, u32[]{:S(2)}) copy-start(bf16[12,128,6,128]{1,3,2,0:T(8,128)(2,1)S(1)} %fusion.4) | copy-start | bytes 7077892
  164.2 7.9 %copy-start.12 = (bf16[12,128,2,128]{1,3,2,0:T(8,128)(2,1)S(1)}, bf16[12,128,2,128]{1,3,2,0:T(8,128)(2,1)}, u32[]{:S(2)}) copy-start(bf16[12,128,2,128]{1,3,2,0:T(8,128)(2,1)} %get-tuple-element.15) | copy-start | bytes 2359300
  165.5 22.9 %collective-permute-start.5 = (bf16[2,128,12,128]{3,1,2,0:T(8,128)(2,1)S(1)}, bf16[2,128,12,128]{3,1,2,0:T(8,128)(2,1)S(1)}, u32[]{:S(2)}, u32[]{:S(2)}) collective-permute-start(bf16[2,128,12,128]{3,1,2,0:T(8,128)(2,1)S(1)} %maximum_bitcast_fusion.3), channel_id=1, source_target_pairs={{0,256},{16,272},{32,288},{48,304},{64,320},{80,336},{96,352},{112... | collective-permute-start | bytes 2359304 | tf_op jit(solution)/shard_map/ppermute | solution.py:27
  172.1 7.5 %copy-start.10 = (bf16[12,128,2,128]{1,3,2,0:T(8,128)(2,1)S(1)}, bf16[12,128,2,128]{1,3,2,0:T(8,128)(2,1)}, u32[]{:S(2)}) copy-start(bf16[12,128,2,128]{1,3,2,0:T(8,128)(2,1)} %get-tuple-element.12) | copy-start | bytes 2359300
  172.4 7.5 %copy-start.4 = (bf16[12,2,128,128]{3,2,0,1:T(8,128)(2,1)}, bf16[12,2,128,128]{3,2,0,1:T(8,128)(2,1)S(1)}, u32[]{:S(2)}) copy-start(bf16[12,2,128,128]{3,2,0,1:T(8,128)(2,1)S(1)} %convolution_convert_fusion) | copy-start | bytes 2359300
  172.4 7.5 %copy-start.11 = (bf16[12,128,2,128]{1,3,2,0:T(8,128)(2,1)S(1)}, bf16[12,128,2,128]{1,3,2,0:T(8,128)(2,1)}, u32[]{:S(2)}) copy-start(bf16[12,128,2,128]{1,3,2,0:T(8,128)(2,1)} %get-tuple-element.14) | copy-start | bytes 2359300
  173.7 46.7 %collective-permute-start.9 = (bf16[1,1,2,128,12,128]{5,3,4,2,1,0:T(8,128)(2,1)}, bf16[1,1,2,128,12,128]{5,3,4,2,1,0:T(8,128)(2,1)}, u32[]{:S(2)}, u32[]{:S(2)}) collective-permute-start(bf16[1,1,2,128,12,128]{5,3,4,2,1,0:T(8,128)(2,1)} %get-tuple-element.17), channel_id=1, source_target_pairs={{1,0},{2,1},{3,2},{4,3},{5,4},{6,5},{7,6},{8,7},{9,8},{10,9},{11,1... | collective-permute-start | bytes 2359304 | tf_op jit(solution)/shard_map/ppermute | solution.py:19
  176.2 45.5 %collective-permute-start.8 = (bf16[1,1,2,128,12,128]{5,3,4,2,1,0:T(8,128)(2,1)}, bf16[1,1,2,128,12,128]{5,3,4,2,1,0:T(8,128)(2,1)}, u32[]{:S(2)}, u32[]{:S(2)}) collective-permute-start(bf16[1,1,2,128,12,128]{5,3,4,2,1,0:T(8,128)(2,1)} %get-tuple-element.16), channel_id=1, source_target_pairs={{0,1},{1,2},{2,3},{3,4},{4,5},{5,6},{6,7},{7,8},{8,9},{9,10},{10,1... | collective-permute-start | bytes 2359304 | tf_op jit(solution)/shard_map/ppermute | solution.py:17
  180.3 20.1 %copy-start.14 = (bf16[12,128,6,128]{1,3,2,0:T(8,128)(2,1)S(1)}, bf16[12,128,6,128]{1,3,2,0:T(8,128)(2,1)}, u32[]{:S(2)}) copy-start(bf16[12,128,6,128]{1,3,2,0:T(8,128)(2,1)} %copy-done.13) | copy-start | bytes 7077892
  190.0 31.7 %collective-permute-start.7 = (bf16[1,1,2,128,12,128]{5,3,4,2,1,0:T(8,128)(2,1)}, bf16[1,1,2,128,12,128]{5,3,4,2,1,0:T(8,128)(2,1)}, u32[]{:S(2)}, u32[]{:S(2)}) collective-permute-start(bf16[1,1,2,128,12,128]{5,3,4,2,1,0:T(8,128)(2,1)} %bitcast.65), channel_id=1, source_target_pairs={{16,0},{32,16},{48,32},{64,48},{80,64},{96,80},{112,96},{128,112},... | collective-permute-start | bytes 2359304 | tf_op jit(solution)/shard_map/ppermute | solution.py:19
  198.5 38.1 %collective-permute-start.6 = (bf16[1,1,2,128,12,128]{5,3,4,2,1,0:T(8,128)(2,1)}, bf16[1,1,2,128,12,128]{5,3,4,2,1,0:T(8,128)(2,1)}, u32[]{:S(2)}, u32[]{:S(2)}) collective-permute-start(bf16[1,1,2,128,12,128]{5,3,4,2,1,0:T(8,128)(2,1)} %bitcast.60), channel_id=1, source_target_pairs={{0,16},{16,32},{32,48},{48,64},{64,80},{80,96},{96,112},{112,128},... | collective-permute-start | bytes 2359304 | tf_op jit(solution)/shard_map/ppermute | solution.py:17
  205.7 30.9 %copy-start.3 = (bf16[12,2,128,128]{3,2,0,1:T(8,128)(2,1)S(1)}, bf16[12,2,128,128]{3,2,0,1:T(8,128)(2,1)}, u32[]{:S(2)}) copy-start(bf16[12,2,128,128]{3,2,0,1:T(8,128)(2,1)} %copy-done.2) | copy-start | bytes 2359300
  205.7 30.9 %copy-start.5 = (bf16[12,2,128,128]{3,2,0,1:T(8,128)(2,1)S(1)}, bf16[12,2,128,128]{3,2,0,1:T(8,128)(2,1)}, u32[]{:S(2)}) copy-start(bf16[12,2,128,128]{3,2,0,1:T(8,128)(2,1)} %copy-done.4) | copy-start | bytes 2359300
  205.7 30.9 %copy-start.9 = (bf16[2,128,12,128]{3,1,2,0:T(8,128)(2,1)S(1)}, bf16[2,128,12,128]{3,1,2,0:T(8,128)(2,1)}, u32[]{:S(2)}) copy-start(bf16[2,128,12,128]{3,1,2,0:T(8,128)(2,1)} %copy-done.8) | copy-start | bytes 2359300
  (5 other events, 11.9 us)
where the time goes:
time: 242 us
  waiting for transfers between devices  142 us (59%)
  starting transfers between devices  45.5 us (19%)
  local copies, waits for them, and re-layouts  24.3 us (10%)
  other arithmetic  14.5 us (6%)
  matrix products  13.9 us (6%)
    ppermute x4, waiting for transfers between devices, with_halo(): lax.ppermute(tail, axis, [(i, (i + 1) % count) for i in range(ends)])  110 us
    ppermute x4, starting transfers between devices, with_halo(): lax.ppermute(head, axis, [((i + 1) % count, i) for i in range(ends)])  28.4 us
    ppermute x4, waiting for transfers between devices, with_halo(): lax.ppermute(head, axis, [((i + 1) % count, i) for i in range(ends)])  23.6 us
    ppermute x4, starting transfers between devices, with_halo(): lax.ppermute(tail, axis, [(i, (i + 1) % count) for i in range(ends)])  9.37 us
    ppermute x2, waiting for transfers between devices, partner_2(): lax.ppermute(x, axis, [(i, i ^ 1 << apart) for i in range(lax.axis_size(a...  7.99 us
    ppermute x2, starting transfers between devices, partner_2(): lax.ppermute(x, axis, [(i, i ^ 1 << apart) for i in range(lax.axis_size(a...  7.8 us
    slice x2, local copies, waits for them, and re-layouts, body(): near_keys = stacked[:, 0].reshape(6, tokens, head_count, DH)  4.91 us
  transfers between devices with their start and end apart: 10, of which 8 were waited for; matrix products, arithmetic and copies ran while one was open for 8% of the time, Pallas kernels for 0%

commit v1 on v0

v1 whole, which is shorter than its diff:
```python
import functools

import jax
import jax.numpy as jnp
from jax import lax
from jax.experimental import pallas as pl
from jax.experimental.pallas import tpu as pltpu
from jax.sharding import PartitionSpec as P

DH = 128
NEG = -1e30
AHEAD = 4
LAG = 3
MESH = pl.DeviceIdType.MESH

OWN, WEST, EAST, MATE, FAR = range(5)


def nt(a, b):
    return lax.dot_general(a, b, (((1,), (1,)), ((), ())), preferred_element_type=jnp.float32)


def nn(a, b):
    return lax.dot_general(a, b, (((1,), (0,)), ((), ())), preferred_element_type=jnp.float32)


def kernel(
    heads, lon, lat,
    q_hbm, k_hbm, v_hbm, g_hbm, nb_hbm, pt_hbm,
    o_hbm, dq_hbm, dk_hbm, dv_hbm,
    buf, st, far_st, pick, hop, out, nb, pt, bias, flag,
    ld_sem, tb_sem, rx_sem, tx_sem, strx_sem, sttx_sem, picktx_sem, hoprx_sem, hoptx_sem, out_sem,
):
    s = lax.axis_index("lon")
    b = lax.axis_index("lat")
    core = s % 2
    odd = b % 2
    mate_b = b + 1 - 2 * odd
    far_b = b - 1 + 2 * odd
    relay_b = b + 2 - 4 * odd
    on_s = s + 1 - 2 * core
    off_s = (s + 2 * core - 1 + lon) % lon
    west_s = (s + lon - 1) % lon
    east_s = (s + 1) % lon
    quarter = lon // 4
    opp = (s + lon // 2) % lon
    opp_w = (opp + lon - 1) % lon
    opp_e = (opp + 1) % lon
    on_slot = 1 + core
    off_slot = 2 - core
    heavy = odd == core
    has_relay = (relay_b >= 0) & (relay_b < lat)
    has_far = (far_b >= 0) & (far_b < lat)
    polar = (b == 0) | (b == lat - 1)
    scale = DH ** -0.5

    def dev(band, strip):
        return {"lat": band, "lon": strip}

    peers = [
        (None, dev(mate_b, s)),
        (None, dev(b, on_s)),
        (None, dev(b, off_s)),
        (has_far, dev(far_b, s)),
        (b + 2 < lat, dev(b + 2, s)),
        (b >= 2, dev(b - 2, s)),
        (heavy, dev(mate_b, off_s)),
        (polar, dev(b, (s + quarter) % lon)),
        (polar, dev(b, (s + lon - quarter) % lon)),
        (polar, dev(b, opp_w)),
        (polar, dev(b, opp)),
        (polar, dev(b, opp_e)),
    ]

    def columns(h):
        return pl.ds(pl.multiple_of(h * DH, DH), DH)

    sources = ((k_hbm, v_hbm), (q_hbm, g_hbm))

    def load(kind, which, h):
        return pltpu.make_async_copy(
            sources[kind][which].at[:, columns(h)], buf.at[kind, OWN, h, which], ld_sem.at[kind, which, h]
        )

    @pl.loop(0, heads)
    def _(h):
        for kind in range(2):
            for which in range(2):
                load(kind, which, h).start()

    tables = (pltpu.make_async_copy(nb_hbm, nb, tb_sem.at[0]), pltpu.make_async_copy(pt_hbm, pt, tb_sem.at[1]))
    for copy in tables:
        copy.start()

    barrier = pltpu.get_barrier_semaphore()
    expected = 0
    for cond, device in peers:
        if cond is None:
            pl.semaphore_signal(barrier, inc=1, device_id=device, device_id_type=MESH)
            expected = expected + 1
        else:
            @pl.when(cond)
            def _():
                pl.semaphore_signal(barrier, inc=1, device_id=device, device_id_type=MESH)
            expected = expected + jnp.where(cond, 1, 0)
    pl.semaphore_wait(barrier, expected)

    def send(src, dst, tx, rx, device):
        return pltpu.make_async_remote_copy(
            src_ref=src, dst_ref=dst, send_sem=tx, recv_sem=rx, device_id=device, device_id_type=MESH
        )

    def chunk(kind, from_slot, to_slot, h, route, device):
        return send(
            buf.at[kind, from_slot, h], buf.at[kind, to_slot, h],
            tx_sem.at[kind, route, h], rx_sem.at[kind, to_slot, h], device,
        )

    def to_mate(kind, h):
        return chunk(kind, OWN, MATE, h, 0, dev(mate_b, s))

    def to_core(kind, h):
        return chunk(kind, OWN, on_slot, h, 1, dev(b, on_s))

    def to_side(kind, h):
        return chunk(kind, OWN, off_slot, h, 2, dev(b, off_s))

    def mate_to_band(kind, h):
        return chunk(kind, MATE, FAR, h, 3, dev(relay_b, s))

    def mate_to_side(kind, h):
        return chunk(kind, MATE, off_slot, h, 4, dev(mate_b, off_s))

    def arrival(kind, slot, h):
        return chunk(kind, slot, slot, h, 0, dev(mate_b, s))

    def around(kind, strip, steps):
        return (strip + (steps * quarter if kind == 0 else lon - steps * quarter)) % lon

    def pick_to_hop(kind, h):
        return send(
            pick.at[kind, h], hop.at[kind, h], picktx_sem.at[kind, h], hoprx_sem.at[kind, h], dev(b, around(kind, s, 1))
        )

    def hop_to_far(kind, h):
        return send(
            hop.at[kind, h], buf.at[kind, FAR, h], hoptx_sem.at[kind, h], rx_sem.at[kind, FAR, h],
            dev(b, around(kind, s, 1)),
        )

    def stat(to_slot, h, route, device):
        return send(st.at[OWN, h], st.at[to_slot, h], sttx_sem.at[route, h], strx_sem.at[to_slot, h], device)

    def stat_sends(h):
        return (
            (None, stat(EAST, h, 0, dev(b, west_s))),
            (None, stat(WEST, h, 1, dev(b, east_s))),
            (None, stat(MATE, h, 2, dev(mate_b, s))),
            (has_far, stat(FAR, h, 3, dev(far_b, s))),
            (polar, stat(FAR, h, 3, dev(b, opp))),
            (polar, stat(6, h, 4, dev(b, opp_w))),
            (polar, stat(5, h, 5, dev(b, opp_e))),
        )

    def guarded(cond, action):
        if cond is None:
            action()
        else:
            pl.when(cond)(action)

    def within(h):
        return (h >= 0) & (h < heads)

    def send_own(kind, h):
        if kind == 0:
            for k in range(2):
                for which in range(2):
                    load(k, which, h).wait()
        to_mate(kind, h).start()
        to_core(kind, h).start()
        pl.when(heavy)(lambda: to_side(kind, h).start())

    def own_sends(t):
        for kind, h in ((0, t + AHEAD), (1, t + AHEAD - LAG)):
            pl.when(within(h))(functools.partial(send_own, kind, h))

    def relay(kind, h):
        arrival(kind, MATE, h).wait_recv()
        pl.when(heavy)(lambda: mate_to_side(kind, h).start())
        pl.when(has_relay)(lambda: mate_to_band(kind, h).start())

    def collect(kind, h):
        arrival(kind, WEST, h).wait_recv()
        arrival(kind, EAST, h).wait_recv()

        @pl.when(polar)
        def _():
            for which in range(2):
                total = buf[kind, OWN, h, which].astype(jnp.float32) * flag[3 * kind, 0:1, :]
                total += buf[kind, WEST, h, which].astype(jnp.float32) * flag[3 * kind + 1, 0:1, :]
                total += buf[kind, EAST, h, which].astype(jnp.float32) * flag[3 * kind + 2, 0:1, :]
                pick[kind, h, which] = total.astype(jnp.bfloat16)
            pick_to_hop(kind, h).start()

    def forward_hop(kind, h):
        pick_to_hop(kind, h).wait_recv()
        hop_to_far(kind, h).start()

    def result(i, h):
        return pltpu.make_async_copy(
            out.at[i, h], (o_hbm, dq_hbm, dk_hbm, dv_hbm)[i].at[:, columns(h)], out_sem.at[i, h]
        )

    def attend(h):
        arrival(0, FAR, h).wait_recv()
        query = buf[1, OWN, h, 0]
        cotan = buf[1, OWN, h, 1]
        keys = buf[0, :, h, 0].reshape(5 * DH, DH)
        values = buf[0, :, h, 1].reshape(5 * DH, DH)
        scores = nt(query, keys) * scale + bias[0, 0:1, :]
        highest = jnp.max(scores, axis=1, keepdims=True)
        grown = jnp.exp(scores - highest)
        total = jnp.sum(grown, axis=1, keepdims=True)
        probability = grown * (1.0 / total)
        attended = nn(probability.astype(jnp.bfloat16), values).astype(jnp.bfloat16)
        delta = jnp.sum(cotan.astype(jnp.float32) * attended.astype(jnp.float32), axis=1, keepdims=True)
        lse = highest + jnp.log(total)
        lane = lax.broadcasted_iota(jnp.int32, (DH, DH), 1)
        both = jnp.where(lane < 4, jnp.broadcast_to(lse, (DH, DH)), jnp.broadcast_to(delta, (DH, DH)))
        st[OWN, h] = jnp.transpose(both)[0:8, :]
        for cond, copy in stat_sends(h):
            guarded(cond, copy.start)
        out[0, h] = attended
        result(0, h).start()
        dprob = nt(cotan, values)
        dscore = (probability * (dprob - delta)).astype(jnp.bfloat16)
        out[1, h] = (nn(dscore, keys) * scale).astype(jnp.bfloat16)
        result(1, h).start()

    def spread(h):
        arrival(1, FAR, h).wait_recv()
        for slot in (WEST, EAST, MATE, FAR):
            stat(slot, h, 0, dev(mate_b, s)).wait_recv()
        pl.when(~polar)(lambda: far_st.__setitem__(Ellipsis, st[FAR, h]))

        @pl.when(polar)
        def _():
            for slot in (5, 6):
                stat(slot, h, 0, dev(mate_b, s)).wait_recv()
            chosen = jnp.where(flag[6, :, :] > 0.5, st[5, h], st[FAR, h])
            far_st[...] = jnp.where(flag[7, :, :] > 0.5, st[6, h], chosen)

        rows = [st[slot, h] for slot in (OWN, WEST, EAST, MATE)] + [far_st[...]]
        shift = bias[1, 0:1, :] - jnp.concatenate([r[0:1, :] for r in rows], axis=1)
        delta = jnp.concatenate([r[4:5, :] for r in rows], axis=1)
        key = buf[0, OWN, h, 0]
        value = buf[0, OWN, h, 1]
        queries = buf[1, :, h, 0].reshape(5 * DH, DH)
        cotans = buf[1, :, h, 1].reshape(5 * DH, DH)
        probability = jnp.exp(nt(key, queries) * scale + shift)
        dscore = (probability * (nt(value, cotans) - delta)).astype(jnp.bfloat16)
        out[3, h] = nn(probability.astype(jnp.bfloat16), cotans).astype(jnp.bfloat16)
        result(3, h).start()
        out[2, h] = (nn(dscore, queries) * scale).astype(jnp.bfloat16)
        result(2, h).start()

    @pl.loop(0, AHEAD)
    def _(t):
        own_sends(t - AHEAD)

    for copy in tables:
        copy.wait()

    ids = [b * lon + s, b * lon + west_s, b * lon + east_s, mate_b * lon + s, far_b * lon + s]
    table = nb[...].astype(jnp.float32)
    lanes = lax.broadcasted_iota(jnp.int32, table.shape, 1)

    def lists(tile, other):
        row = jnp.sum(jnp.where(lanes == tile, table, 0.0), axis=1, keepdims=True)
        hit = jnp.where(row == other.astype(jnp.float32), 1.0, 0.0)
        return jnp.max(hit, axis=0, keepdims=True)

    def as_bias(parts):
        polar_one = jnp.where(polar, 1.0, 0.0)
        parts[FAR] = jnp.maximum(parts[FAR], polar_one)
        whole = jnp.concatenate([jnp.broadcast_to(p, (8, DH)) for p in parts], axis=1)
        return jnp.where(whole > 0.5, 0.0, NEG)

    bias[0] = as_bias([lists(ids[0], other) for other in ids])
    bias[1] = as_bias([lists(other, ids[0]) for other in ids])

    @pl.when(polar)
    def _():
        across = pt[...].astype(jnp.float32)
        strip_of = lax.broadcasted_iota(jnp.int32, across.shape, 1)
        row_of = lax.broadcasted_iota(jnp.int32, across.shape, 0)
        mine = jnp.where(b == 0, 0, 1)

        def partner_is(strip, other):
            here = jnp.where((row_of == mine) & (strip_of == strip), across, 0.0)
            value = jnp.sum(jnp.sum(here, axis=1, keepdims=True), axis=0, keepdims=True)
            return jnp.broadcast_to(jnp.where(value == other.astype(jnp.float32), 1.0, 0.0), (8, DH))

        pairs = ((partner_is(opp, west_s), partner_is(opp, east_s)), (partner_is(west_s, opp), partner_is(east_s, opp)))
        for kind, (west, east) in enumerate(pairs):
            flag[3 * kind] = 1.0 - west - east
            flag[3 * kind + 1] = west
            flag[3 * kind + 2] = east
        flag[6] = partner_is(opp_w, s)
        flag[7] = partner_is(opp_e, s)

    late = jnp.where(polar, 2, 0)

    @pl.loop(0, heads + LAG + 2)
    def _(t):
        own_sends(t)
        now = ((0, t), (1, t - LAG))
        for kind, h in now:
            pl.when(within(h))(functools.partial(relay, kind, h))
        for kind, h in now:
            pl.when(within(h))(functools.partial(collect, kind, h))
        for kind, h in now:
            pl.when(polar & within(h - 1))(functools.partial(forward_hop, kind, h - 1))
        pl.when(within(t - late))(lambda: attend(t - late))
        pl.when(within(t - late - LAG))(lambda: spread(t - late - LAG))

    @pl.loop(0, heads)
    def _(h):
        for kind in range(2):
            to_mate(kind, h).wait_send()
            to_core(kind, h).wait_send()

            @pl.when(heavy)
            def _():
                to_side(kind, h).wait_send()
                mate_to_side(kind, h).wait_send()

            pl.when(has_relay)(lambda: mate_to_band(kind, h).wait_send())

            @pl.when(polar)
            def _():
                pick_to_hop(kind, h).wait_send()
                hop_to_far(kind, h).wait_send()

        for cond, copy in stat_sends(h):
            guarded(cond, copy.wait_send)
        for i in range(4):
            result(i, h).wait()


def body(queries, keys, values, out_grad, neighbours, partner):
    lon = lax.axis_size("lon")
    lat = lax.axis_size("lat")
    shape = queries.shape
    tokens = shape[0] * shape[1]
    width = shape[2]
    heads = width // DH
    flat = [a.reshape(tokens, width) for a in (queries, keys, values, out_grad)]
    anywhere = pl.BlockSpec(memory_space=pl.ANY)
    bf16 = jnp.bfloat16
    f32 = jnp.float32
    dma = pltpu.SemaphoreType.DMA
    tile = (DH, DH)
    results = pl.pallas_call(
        functools.partial(kernel, heads, lon, lat),
        out_shape=[jax.ShapeDtypeStruct((tokens, width), bf16)] * 4,
        in_specs=[anywhere] * 6,
        out_specs=[anywhere] * 4,
        scratch_shapes=[
            pltpu.VMEM((2, 5, heads, 2) + tile, bf16),
            pltpu.VMEM((7, heads, 8, DH), f32),
            pltpu.VMEM((8, DH), f32),
            pltpu.VMEM((2, heads, 2) + tile, bf16),
            pltpu.VMEM((2, heads, 2) + tile, bf16),
            pltpu.VMEM((4, heads) + tile, bf16),
            pltpu.VMEM(neighbours.shape[::-1], jnp.int32),
            pltpu.VMEM(partner.shape, jnp.int32),
            pltpu.VMEM((2, 8, 5 * DH), f32),
            pltpu.VMEM((8, 8, DH), f32),
            dma((2, 2, heads)),
            dma((2,)),
            dma((2, 5, heads)),
            dma((2, 5, heads)),
            dma((7, heads)),
            dma((6, heads)),
            dma((2, heads)),
            dma((2, heads)),
            dma((2, heads)),
            dma((4, heads)),
        ],
        compiler_params=pltpu.CompilerParams(
            collective_id=0, has_side_effects=True, vmem_limit_bytes=48 * 1024 * 1024
        ),
        name="tile_attention",
    )(*flat, neighbours.T, partner)
    return tuple(r.reshape(shape) for r in results)


def solution(mesh):
    tiled = P("lat", "lon", None)
    return jax.shard_map(
        body,
        mesh=mesh,
        in_specs=(tiled, tiled, tiled, tiled, P(), P()),
        out_specs=(tiled, tiled, tiled, tiled),
        check_vma=False,
    )
```

time: 242 us -> 144 us (0.60)
  the two profiles are of different devices: /device:TPU:24 before, /device:TPU:4 now
where the time goes in v1:
time: 144 us; the launch traced here: 143 us
  Pallas kernels  134 us (93%)
  local copies, waits for them, and re-layouts  8.35 us (6%)
    pallas_call x1, Pallas kernels, body(): pl.pallas_call(functools.partial(kernel, heads, lon, lat), out_shape=[jax...  134 us
    unnamed x16, local copies, waits for them, and re-layouts  8.35 us

profile of v1, /device:TPU:4, one launch (start us, length us, event | category | flops | bytes accessed | tf_op | source)
XLA Modules:
  0.0 143.3 jit_solution(10658796635155484630)
XLA Ops:
  0.6 0.0 copy-start.5
  0.6 0.7 copy-done.5
  1.3 0.0 copy-start
  1.3 1.0 copy-done
  2.3 0.0 copy-start.1
  2.3 1.0 copy-done.1
  3.3 0.0 copy-start.2
  3.3 1.0 copy-done.2
  4.3 0.0 copy-start.3
  4.3 1.0 copy-done.3
  5.3 0.0 copy-start.4
  5.3 0.7 copy-done.4
  6.0 134.3 %tile_attention.1 = (bf16[128,1536]{1,0:T(8,128)(2,1)S(1)}, bf16[128,1536]{1,0:T(8,128)(2,1)S(1)}, bf16[128,1536]{1,0:T(8,128)(2,1)S(1)}, bf16[128,1536]{1,0:T(8,128)(2,1)S(1)}) custom-call(bf16[128,1536]{1,0:T(8,128)(2,1)S(1)} %bitcast.13, bf16[128,1536]{1,0:T(8,128)(2,1)S(1)} %bitcast.14, bf16[128,1536]{1,0:T(8,128)(2,1)S(1)} %bitcast.15, ...), custom_call_target="tpu_custom_call" | custom-call | tf_op jit(solution)/shard_map/tile_attention/pallas_call | solution.py:364
  140.3 0.7 copy.14
  141.1 0.7 copy.15
  141.8 0.7 copy.16
  142.6 0.7 copy.17
Async XLA Ops:
  0.6 0.7 copy-start.5
  1.3 1.0 copy-start
  2.3 1.0 copy-start.1
  3.3 1.0 copy-start.2
  4.3 1.0 copy-start.3
  5.3 0.7 copy-start.4

commit v2 on v1

--- a/solution.py
+++ b/solution.py
@@ -9,8 +9,10 @@
 
 DH = 128
 NEG = -1e30
-AHEAD = 4
+AHEAD = 5
+SIDE = 2
 LAG = 3
+LATE = 2
 MESH = pl.DeviceIdType.MESH
 
 OWN, WEST, EAST, MATE, FAR = range(5)
@@ -28,8 +30,8 @@
     heads, lon, lat,
     q_hbm, k_hbm, v_hbm, g_hbm, nb_hbm, pt_hbm,
     o_hbm, dq_hbm, dk_hbm, dv_hbm,
-    buf, st, far_st, pick, hop, out, nb, pt, bias, flag,
-    ld_sem, tb_sem, rx_sem, tx_sem, strx_sem, sttx_sem, picktx_sem, hoprx_sem, hoptx_sem, out_sem,
+    buf, st, far_st, pick, out, nb, pt, bias, flag,
+    ld_sem, tb_sem, rx_sem, tx_sem, strx_sem, sttx_sem, picktx_sem, out_sem,
 ):
     s = lax.axis_index("lon")
     b = lax.axis_index("lat")
@@ -42,7 +44,6 @@
     off_s = (s + 2 * core - 1 + lon) % lon
     west_s = (s + lon - 1) % lon
     east_s = (s + 1) % lon
-    quarter = lon // 4
     opp = (s + lon // 2) % lon
     opp_w = (opp + lon - 1) % lon
     opp_e = (opp + 1) % lon
@@ -65,8 +66,6 @@
         (b + 2 < lat, dev(b + 2, s)),
         (b >= 2, dev(b - 2, s)),
         (heavy, dev(mate_b, off_s)),
-        (polar, dev(b, (s + quarter) % lon)),
-        (polar, dev(b, (s + lon - quarter) % lon)),
         (polar, dev(b, opp_w)),
         (polar, dev(b, opp)),
         (polar, dev(b, opp_e)),
@@ -134,18 +133,9 @@
     def arrival(kind, slot, h):
         return chunk(kind, slot, slot, h, 0, dev(mate_b, s))
 
-    def around(kind, strip, steps):
-        return (strip + (steps * quarter if kind == 0 else lon - steps * quarter)) % lon
-
-    def pick_to_hop(kind, h):
+    def pick_to_far(kind, h):
         return send(
-            pick.at[kind, h], hop.at[kind, h], picktx_sem.at[kind, h], hoprx_sem.at[kind, h], dev(b, around(kind, s, 1))
-        )
-
-    def hop_to_far(kind, h):
-        return send(
-            hop.at[kind, h], buf.at[kind, FAR, h], hoptx_sem.at[kind, h], rx_sem.at[kind, FAR, h],
-            dev(b, around(kind, s, 1)),
+            pick.at[kind, h], buf.at[kind, FAR, h], picktx_sem.at[kind, h], rx_sem.at[kind, FAR, h], dev(b, opp)
         )
 
     def stat(to_slot, h, route, device):
@@ -178,13 +168,13 @@
                     load(k, which, h).wait()
         to_mate(kind, h).start()
         to_core(kind, h).start()
-        pl.when(heavy)(lambda: to_side(kind, h).start())
 
     def own_sends(t):
         for kind, h in ((0, t + AHEAD), (1, t + AHEAD - LAG)):
             pl.when(within(h))(functools.partial(send_own, kind, h))
 
     def relay(kind, h):
+        pl.when(heavy)(lambda: to_side(kind, h).start())
         arrival(kind, MATE, h).wait_recv()
         pl.when(heavy)(lambda: mate_to_side(kind, h).start())
         pl.when(has_relay)(lambda: mate_to_band(kind, h).start())
@@ -200,11 +190,7 @@
                 total += buf[kind, WEST, h, which].astype(jnp.float32) * flag[3 * kind + 1, 0:1, :]
                 total += buf[kind, EAST, h, which].astype(jnp.float32) * flag[3 * kind + 2, 0:1, :]
                 pick[kind, h, which] = total.astype(jnp.bfloat16)
-            pick_to_hop(kind, h).start()
-
-    def forward_hop(kind, h):
-        pick_to_hop(kind, h).wait_recv()
-        hop_to_far(kind, h).start()
+            pick_to_far(kind, h).start()
 
     def result(i, h):
         return pltpu.make_async_copy(
@@ -264,9 +250,17 @@
         out[2, h] = (nn(dscore, queries) * scale).astype(jnp.bfloat16)
         result(2, h).start()
 
+    def relays(t):
+        for kind, h in ((0, t + SIDE), (1, t + SIDE - LAG)):
+            pl.when(within(h))(functools.partial(relay, kind, h))
+
     @pl.loop(0, AHEAD)
     def _(t):
         own_sends(t - AHEAD)
+
+    @pl.loop(0, SIDE)
+    def _(t):
+        relays(t - SIDE)
 
     for copy in tables:
         copy.wait()
@@ -309,18 +303,14 @@
         flag[6] = partner_is(opp_w, s)
         flag[7] = partner_is(opp_e, s)
 
-    late = jnp.where(polar, 2, 0)
-
-    @pl.loop(0, heads + LAG + 2)
+    late = jnp.where(polar, LATE, 0)
+
+    @pl.loop(0, heads + LAG + LATE)
     def _(t):
         own_sends(t)
-        now = ((0, t), (1, t - LAG))
-        for kind, h in now:
-            pl.when(within(h))(functools.partial(relay, kind, h))
-        for kind, h in now:
+        relays(t)
+        for kind, h in ((0, t), (1, t - LAG)):
             pl.when(within(h))(functools.partial(collect, kind, h))
-        for kind, h in now:
-            pl.when(polar & within(h - 1))(functools.partial(forward_hop, kind, h - 1))
         pl.when(within(t - late))(lambda: attend(t - late))
         pl.when(within(t - late - LAG))(lambda: spread(t - late - LAG))
 
@@ -337,10 +327,7 @@
 
             pl.when(has_relay)(lambda: mate_to_band(kind, h).wait_send())
 
-            @pl.when(polar)
-            def _():
-                pick_to_hop(kind, h).wait_send()
-                hop_to_far(kind, h).wait_send()
+            pl.when(polar)(lambda: pick_to_far(kind, h).wait_send())
 
         for cond, copy in stat_sends(h):
             guarded(cond, copy.wait_send)
@@ -364,13 +351,12 @@
     results = pl.pallas_call(
         functools.partial(kernel, heads, lon, lat),
         out_shape=[jax.ShapeDtypeStruct((tokens, width), bf16)] * 4,
-        in_specs=[anywhere] * 6,
+        in_specs=[pl.BlockSpec(memory_space=pltpu.HBM)] * 6,
         out_specs=[anywhere] * 4,
         scratch_shapes=[
             pltpu.VMEM((2, 5, heads, 2) + tile, bf16),
             pltpu.VMEM((7, heads, 8, DH), f32),
             pltpu.VMEM((8, DH), f32),
-            pltpu.VMEM((2, heads, 2) + tile, bf16),
             pltpu.VMEM((2, heads, 2) + tile, bf16),
             pltpu.VMEM((4, heads) + tile, bf16),
             pltpu.VMEM(neighbours.shape[::-1], jnp.int32),
@@ -384,12 +370,10 @@
             dma((7, heads)),
             dma((6, heads)),
             dma((2, heads)),
-            dma((2, heads)),
-            dma((2, heads)),
             dma((4, heads)),
         ],
         compiler_params=pltpu.CompilerParams(
-            collective_id=0, has_side_effects=True, vmem_limit_bytes=48 * 1024 * 1024
+            collective_id=0, has_side_effects=True, vmem_limit_bytes=63 * 1024 * 1024
         ),
         name="tile_attention",
     )(*flat, neighbours.T, partner)

time: 144 us -> 93.1 us (0.65)
  Pallas kernels: 134 us -> 87.3 us
  local copies, waits for them, and re-layouts: 8.35 us -> 4.84 us
    pallas_call x1, Pallas kernels: 134 us -> 87.3 us  [body(): pl.pallas_call(functools.partial(kernel, heads, lon, lat), out_shape=[jax...]
    unnamed x16 -> x10, local copies, waits for them, and re-layouts: 8.35 us -> 4.84 us
where the time goes in v2:
time: 93.1 us; the launch traced here: 92.8 us
  Pallas kernels  87.3 us (94%)
  local copies, waits for them, and re-layouts  4.84 us (5%)
    pallas_call x1, Pallas kernels, body(): pl.pallas_call(functools.partial(kernel, heads, lon, lat), out_shape=[jax...  87.3 us
    unnamed x10, local copies, waits for them, and re-layouts  4.84 us

profile of v2, /device:TPU:4, one launch (start us, length us, event | category | flops | bytes accessed | tf_op | source)
XLA Modules:
  0.0 92.8 jit_solution(11678826295453346693)
XLA Ops:
  0.6 87.3 %tile_attention.1 = (bf16[128,1536]{1,0:T(8,128)(2,1)}, bf16[128,1536]{1,0:T(8,128)(2,1)}, bf16[128,1536]{1,0:T(8,128)(2,1)}, bf16[128,1536]{1,0:T(8,128)(2,1)}) custom-call(bf16[128,1536]{1,0:T(8,128)(2,1)} %bitcast.13, bf16[128,1536]{1,0:T(8,128)(2,1)} %bitcast.14, bf16[128,1536]{1,0:T(8,128)(2,1)} %bitcast.15, bf16[128,1536]{1,0:T(8,128)(2,1)} %bitcast.16, ...), custom_call_target="tpu_custom_call" | custom-call | tf_op jit(solution)/shard_map/tile_attention/pallas_call | solution.py:351
  87.9 0.0 copy-start.2
  87.9 1.8 %copy.14 = bf16[8,16,1536]{2,1,0:T(8,128)(2,1)} copy(bf16[8,16,1536]{2,1,0:T(8,128)(2,1)} %bitcast.12) | data formatting | bytes 786432
  89.7 0.0 copy-done.2
  89.8 0.0 copy-start.1
  89.8 0.7 copy.15
  90.5 0.4 copy-done.1
  90.9 0.0 copy-start
  90.9 0.7 copy.16
  91.6 0.4 copy-done
  92.0 0.7 copy.17
Async XLA Ops:
  87.9 1.8 %copy-start.2 = (bf16[128,1536]{1,0:T(8,128)(2,1)S(1)}, bf16[128,1536]{1,0:T(8,128)(2,1)}, u32[]{:S(2)}) copy-start(bf16[128,1536]{1,0:T(8,128)(2,1)} %get-tuple-element.9) | copy-start | bytes 1179652
  89.8 1.1 %copy-start.1 = (bf16[128,1536]{1,0:T(8,128)(2,1)S(1)}, bf16[128,1536]{1,0:T(8,128)(2,1)}, u32[]{:S(2)}) copy-start(bf16[128,1536]{1,0:T(8,128)(2,1)} %get-tuple-element.10) | copy-start | bytes 1179652
  90.9 1.1 %copy-start = (bf16[128,1536]{1,0:T(8,128)(2,1)S(1)}, bf16[128,1536]{1,0:T(8,128)(2,1)}, u32[]{:S(2)}) copy-start(bf16[128,1536]{1,0:T(8,128)(2,1)} %get-tuple-element.11) | copy-start | bytes 1179652

commit v3 on v2

--- a/solution.py
+++ b/solution.py
@@ -11,8 +11,9 @@
 NEG = -1e30
 AHEAD = 5
 SIDE = 2
-LAG = 3
-LATE = 2
+LAG = 8
+LATE = 4
+FAR_LATE = 6
 MESH = pl.DeviceIdType.MESH
 
 OWN, WEST, EAST, MATE, FAR = range(5)
@@ -29,9 +30,9 @@
 def kernel(
     heads, lon, lat,
     q_hbm, k_hbm, v_hbm, g_hbm, nb_hbm, pt_hbm,
-    o_hbm, dq_hbm, dk_hbm, dv_hbm,
-    buf, st, far_st, pick, out, nb, pt, bias, flag,
-    ld_sem, tb_sem, rx_sem, tx_sem, strx_sem, sttx_sem, picktx_sem, out_sem,
+    out_o, out_dq, out_dk, out_dv,
+    buf, st, far_st, near, pick, nb, pt, bias, flag,
+    ld_sem, tb_sem, rx_sem, tx_sem, strx_sem, sttx_sem, picktx_sem,
 ):
     s = lax.axis_index("lon")
     b = lax.axis_index("lat")
@@ -192,11 +193,6 @@
                 pick[kind, h, which] = total.astype(jnp.bfloat16)
             pick_to_far(kind, h).start()
 
-    def result(i, h):
-        return pltpu.make_async_copy(
-            out.at[i, h], (o_hbm, dq_hbm, dk_hbm, dv_hbm)[i].at[:, columns(h)], out_sem.at[i, h]
-        )
-
     def attend(h):
         arrival(0, FAR, h).wait_recv()
         query = buf[1, OWN, h, 0]
@@ -216,17 +212,32 @@
         st[OWN, h] = jnp.transpose(both)[0:8, :]
         for cond, copy in stat_sends(h):
             guarded(cond, copy.start)
-        out[0, h] = attended
-        result(0, h).start()
+        out_o[:, columns(h)] = attended
         dprob = nt(cotan, values)
         dscore = (probability * (dprob - delta)).astype(jnp.bfloat16)
-        out[1, h] = (nn(dscore, keys) * scale).astype(jnp.bfloat16)
-        result(1, h).start()
-
-    def spread(h):
+        out_dq[:, columns(h)] = (nn(dscore, keys) * scale).astype(jnp.bfloat16)
+
+    def terms(h, first, count, rows):
+        def row(i):
+            return jnp.concatenate([r[i : i + 1, :] for r in rows], axis=1)
+
+        shift = bias[1, 0:1, first * DH : (first + count) * DH] - row(0)
+        queries = buf[1, first : first + count, h, 0].reshape(count * DH, DH)
+        cotans = buf[1, first : first + count, h, 1].reshape(count * DH, DH)
+        probability = jnp.exp(nt(buf[0, OWN, h, 0], queries) * scale + shift)
+        dscore = (probability * (nt(buf[0, OWN, h, 1], cotans) - row(4))).astype(jnp.bfloat16)
+        return nn(dscore, queries), nn(probability.astype(jnp.bfloat16), cotans)
+
+    def spread_near(h):
+        for slot in (WEST, EAST, MATE):
+            stat(slot, h, 0, dev(mate_b, s)).wait_recv()
+        key_sum, value_sum = terms(h, OWN, 4, [st[slot, h] for slot in (OWN, WEST, EAST, MATE)])
+        near[h % 7, 0] = key_sum
+        near[h % 7, 1] = value_sum
+
+    def spread_far(h):
         arrival(1, FAR, h).wait_recv()
-        for slot in (WEST, EAST, MATE, FAR):
-            stat(slot, h, 0, dev(mate_b, s)).wait_recv()
+        stat(FAR, h, 0, dev(mate_b, s)).wait_recv()
         pl.when(~polar)(lambda: far_st.__setitem__(Ellipsis, st[FAR, h]))
 
         @pl.when(polar)
@@ -236,19 +247,14 @@
             chosen = jnp.where(flag[6, :, :] > 0.5, st[5, h], st[FAR, h])
             far_st[...] = jnp.where(flag[7, :, :] > 0.5, st[6, h], chosen)
 
-        rows = [st[slot, h] for slot in (OWN, WEST, EAST, MATE)] + [far_st[...]]
-        shift = bias[1, 0:1, :] - jnp.concatenate([r[0:1, :] for r in rows], axis=1)
-        delta = jnp.concatenate([r[4:5, :] for r in rows], axis=1)
-        key = buf[0, OWN, h, 0]
-        value = buf[0, OWN, h, 1]
-        queries = buf[1, :, h, 0].reshape(5 * DH, DH)
-        cotans = buf[1, :, h, 1].reshape(5 * DH, DH)
-        probability = jnp.exp(nt(key, queries) * scale + shift)
-        dscore = (probability * (nt(value, cotans) - delta)).astype(jnp.bfloat16)
-        out[3, h] = nn(probability.astype(jnp.bfloat16), cotans).astype(jnp.bfloat16)
-        result(3, h).start()
-        out[2, h] = (nn(dscore, queries) * scale).astype(jnp.bfloat16)
-        result(2, h).start()
+        key_sum, value_sum = terms(h, FAR, 1, [far_st[...]])
+        out_dk[:, columns(h)] = ((near[h % 7, 0] + key_sum) * scale).astype(jnp.bfloat16)
+        out_dv[:, columns(h)] = (near[h % 7, 1] + value_sum).astype(jnp.bfloat16)
+
+    def spread(t):
+        pl.when(within(t - LAG))(lambda: spread_near(t - LAG))
+        late = jnp.where(polar, FAR_LATE, 0)
+        pl.when(within(t - LAG - late))(lambda: spread_far(t - LAG - late))
 
     def relays(t):
         for kind, h in ((0, t + SIDE), (1, t + SIDE - LAG)):
@@ -305,14 +311,16 @@
 
     late = jnp.where(polar, LATE, 0)
 
-    @pl.loop(0, heads + LAG + LATE)
+    @pl.loop(0, heads + LAG + FAR_LATE)
     def _(t):
-        own_sends(t)
-        relays(t)
-        for kind, h in ((0, t), (1, t - LAG)):
-            pl.when(within(h))(functools.partial(collect, kind, h))
-        pl.when(within(t - late))(lambda: attend(t - late))
-        pl.when(within(t - late - LAG))(lambda: spread(t - late - LAG))
+        for kind, lag in ((0, 0), (1, LAG)):
+            pl.when(within(t + AHEAD - lag))(lambda: send_own(kind, t + AHEAD - lag))
+            pl.when(within(t + SIDE - lag))(lambda: relay(kind, t + SIDE - lag))
+            pl.when(within(t - lag))(lambda: collect(kind, t - lag))
+            if kind == 0:
+                pl.when(within(t - late))(lambda: attend(t - late))
+            else:
+                spread(t)
 
     @pl.loop(0, heads)
     def _(h):
@@ -331,8 +339,14 @@
 
         for cond, copy in stat_sends(h):
             guarded(cond, copy.wait_send)
-        for i in range(4):
-            result(i, h).wait()
+
+
+def store(*refs):
+    copies = [pltpu.make_async_copy(refs[i], refs[4 + i], refs[8].at[i]) for i in range(4)]
+    for copy in copies:
+        copy.start()
+    for copy in copies:
+        copy.wait()
 
 
 def body(queries, keys, values, out_grad, neighbours, partner):
@@ -343,7 +357,6 @@
     width = shape[2]
     heads = width // DH
     flat = [a.reshape(tokens, width) for a in (queries, keys, values, out_grad)]
-    anywhere = pl.BlockSpec(memory_space=pl.ANY)
     bf16 = jnp.bfloat16
     f32 = jnp.float32
     dma = pltpu.SemaphoreType.DMA
@@ -352,13 +365,13 @@
         functools.partial(kernel, heads, lon, lat),
         out_shape=[jax.ShapeDtypeStruct((tokens, width), bf16)] * 4,
         in_specs=[pl.BlockSpec(memory_space=pltpu.HBM)] * 6,
-        out_specs=[anywhere] * 4,
+        out_specs=[pl.BlockSpec(memory_space=pltpu.VMEM)] * 4,
         scratch_shapes=[
             pltpu.VMEM((2, 5, heads, 2) + tile, bf16),
             pltpu.VMEM((7, heads, 8, DH), f32),
             pltpu.VMEM((8, DH), f32),
+            pltpu.VMEM((7, 2) + tile, f32),
             pltpu.VMEM((2, heads, 2) + tile, bf16),
-            pltpu.VMEM((4, heads) + tile, bf16),
             pltpu.VMEM(neighbours.shape[::-1], jnp.int32),
             pltpu.VMEM(partner.shape, jnp.int32),
             pltpu.VMEM((2, 8, 5 * DH), f32),
@@ -370,14 +383,21 @@
             dma((7, heads)),
             dma((6, heads)),
             dma((2, heads)),
-            dma((4, heads)),
         ],
         compiler_params=pltpu.CompilerParams(
-            collective_id=0, has_side_effects=True, vmem_limit_bytes=63 * 1024 * 1024
+            collective_id=0, has_side_effects=True, vmem_limit_bytes=48 * 1024 * 1024
         ),
         name="tile_attention",
-    )(*flat, neighbours.T, partner)
-    return tuple(r.reshape(shape) for r in results)
+    )(*[pltpu.with_memory_space_constraint(a, pltpu.HBM) for a in (*flat, neighbours.T, partner)])
+    finished = pl.pallas_call(
+        store,
+        out_shape=[jax.ShapeDtypeStruct((tokens, width), bf16)] * 4,
+        in_specs=[pl.BlockSpec(memory_space=pl.ANY)] * 4,
+        out_specs=[pl.BlockSpec(memory_space=pltpu.HBM)] * 4,
+        scratch_shapes=[dma((4,))],
+        name="store_results",
+    )(*[pltpu.with_memory_space_constraint(r, pltpu.VMEM) for r in results])
+    return tuple(r.reshape(shape) for r in finished)
 
 
 def solution(mesh):

time: 93.1 us -> 82.7 us (0.89)
  the two profiles are of different devices: /device:TPU:4 before, /device:TPU:120 now
where the time goes in v3:
time: 82.7 us; the launch traced here: 82.5 us
  Pallas kernels  81.9 us (99%)
    pallas_call x1, Pallas kernels, body(): pl.pallas_call(functools.partial(kernel, heads, lon, lat), out_shape=[jax...  80.7 us

profile of v3, /device:TPU:120, one launch (start us, length us, event | category | flops | bytes accessed | tf_op | source)
XLA Modules:
  0.0 82.5 jit_solution(9943016888156166264)
XLA Ops:
  0.6 80.7 %tile_attention.1 = (bf16[128,1536]{1,0:T(8,128)(2,1)S(1)}, bf16[128,1536]{1,0:T(8,128)(2,1)S(1)}, bf16[128,1536]{1,0:T(8,128)(2,1)S(1)}, bf16[128,1536]{1,0:T(8,128)(2,1)S(1)}) custom-call(bf16[128,1536]{1,0:T(8,128)(2,1)} %bitcast.9, bf16[128,1536]{1,0:T(8,128)(2,1)} %bitcast.10, bf16[128,1536]{1,0:T(8,128)(2,1)} %bitcast.11, bf16[128,1536]{1,0:T(8,128)(2,1)} %bitcast.12, ...), custom_call_target="tpu_custom_call" | custom-call | tf_op jit(solution)/shard_map/tile_attention/pallas_call | solution.py:364
  81.4 1.2 %store_results.1 = (bf16[128,1536]{1,0:T(8,128)(2,1)}, bf16[128,1536]{1,0:T(8,128)(2,1)}, bf16[128,1536]{1,0:T(8,128)(2,1)}, bf16[128,1536]{1,0:T(8,128)(2,1)}) custom-call(bf16[128,1536]{1,0:T(8,128)(2,1)S(1)} %get-tuple-element.12.refs_0_, bf16[128,1536]{1,0:T(8,128)(2,1)S(1)} %get-tuple-element.13.refs_1_, ...), custom_call_target="tpu_custom_call" | custom-call | tf_op jit(solution)/shard_map/store_results/pallas_call | solution.py:392

commit v4 on v3

--- a/solution.py
+++ b/solution.py
@@ -9,11 +9,11 @@
 
 DH = 128
 NEG = -1e30
-AHEAD = 5
+AHEAD = 4
 SIDE = 2
 LAG = 8
-LATE = 4
-FAR_LATE = 6
+LATE = 5
+FAR_LATE = 7
 MESH = pl.DeviceIdType.MESH
 
 OWN, WEST, EAST, MATE, FAR = range(5)
@@ -232,8 +232,8 @@
         for slot in (WEST, EAST, MATE):
             stat(slot, h, 0, dev(mate_b, s)).wait_recv()
         key_sum, value_sum = terms(h, OWN, 4, [st[slot, h] for slot in (OWN, WEST, EAST, MATE)])
-        near[h % 7, 0] = key_sum
-        near[h % 7, 1] = value_sum
+        near[h % 8, 0] = key_sum
+        near[h % 8, 1] = value_sum
 
     def spread_far(h):
         arrival(1, FAR, h).wait_recv()
@@ -248,8 +248,8 @@
             far_st[...] = jnp.where(flag[7, :, :] > 0.5, st[6, h], chosen)
 
         key_sum, value_sum = terms(h, FAR, 1, [far_st[...]])
-        out_dk[:, columns(h)] = ((near[h % 7, 0] + key_sum) * scale).astype(jnp.bfloat16)
-        out_dv[:, columns(h)] = (near[h % 7, 1] + value_sum).astype(jnp.bfloat16)
+        out_dk[:, columns(h)] = ((near[h % 8, 0] + key_sum) * scale).astype(jnp.bfloat16)
+        out_dv[:, columns(h)] = (near[h % 8, 1] + value_sum).astype(jnp.bfloat16)
 
     def spread(t):
         pl.when(within(t - LAG))(lambda: spread_near(t - LAG))
@@ -370,7 +370,7 @@
             pltpu.VMEM((2, 5, heads, 2) + tile, bf16),
             pltpu.VMEM((7, heads, 8, DH), f32),
             pltpu.VMEM((8, DH), f32),
-            pltpu.VMEM((7, 2) + tile, f32),
+            pltpu.VMEM((8, 2) + tile, f32),
             pltpu.VMEM((2, heads, 2) + tile, bf16),
             pltpu.VMEM(neighbours.shape[::-1], jnp.int32),
             pltpu.VMEM(partner.shape, jnp.int32),

time: 82.7 us -> 82.4 us (level)
  no operation moved by 1% of the time
where the time goes in v4:
time: 82.4 us; the launch traced here: 82.2 us
  Pallas kernels  81.6 us (99%)
    pallas_call x1, Pallas kernels, body(): pl.pallas_call(functools.partial(kernel, heads, lon, lat), out_shape=[jax...  80.4 us

profile of v4, /device:TPU:120, one launch (start us, length us, event | category | flops | bytes accessed | tf_op | source)
XLA Modules:
  0.0 82.2 jit_solution(17590864053676245040)
XLA Ops:
  0.6 80.4 %tile_attention.1 = (bf16[128,1536]{1,0:T(8,128)(2,1)S(1)}, bf16[128,1536]{1,0:T(8,128)(2,1)S(1)}, bf16[128,1536]{1,0:T(8,128)(2,1)S(1)}, bf16[128,1536]{1,0:T(8,128)(2,1)S(1)}) custom-call(bf16[128,1536]{1,0:T(8,128)(2,1)} %bitcast.9, bf16[128,1536]{1,0:T(8,128)(2,1)} %bitcast.10, bf16[128,1536]{1,0:T(8,128)(2,1)} %bitcast.11, bf16[128,1536]{1,0:T(8,128)(2,1)} %bitcast.12, ...), custom_call_target="tpu_custom_call" | custom-call | tf_op jit(solution)/shard_map/tile_attention/pallas_call | solution.py:364
  81.1 1.2 %store_results.1 = (bf16[128,1536]{1,0:T(8,128)(2,1)}, bf16[128,1536]{1,0:T(8,128)(2,1)}, bf16[128,1536]{1,0:T(8,128)(2,1)}, bf16[128,1536]{1,0:T(8,128)(2,1)}) custom-call(bf16[128,1536]{1,0:T(8,128)(2,1)S(1)} %get-tuple-element.12.refs_0_, bf16[128,1536]{1,0:T(8,128)(2,1)S(1)} %get-tuple-element.13.refs_1_, ...), custom_call_target="tpu_custom_call" | custom-call | tf_op jit(solution)/shard_map/store_results/pallas_call | solution.py:392
